TPU v7x, 32 devices: a whole 2x2x4 slice. The times are simulated.
32 devices in a mesh: section: 4 (over y, x), ctx: 4 (over z), tp: 2 (over core).
Axes of the slice: x: 2, y: 2, z: 4, core: 2. Of those that a mesh axis runs over, the one named last changes fastest.
Arguments:
- queries: bfloat16 [2048, 8, 8, 128], P('ctx', 'tp', 'section'), may hold values from -44 to 44
- key_states: bfloat16 [2048, 8, 128], P('ctx', 'tp'), may hold values from -4 to 4
- value_states: bfloat16 [2048, 8, 128], P('ctx', 'tp'), may hold values from -6 to 6
- out_grad: bfloat16 [2048, 8, 8, 128], P('ctx', 'tp', 'section'), may hold values from -6 to 6
- band_offsets: int32 [16, 3], replicated, may hold values from -1 to 4, as said below
- global_blocks: int32 [16, 4], replicated, may hold values from -1 to 8, as said below
Outputs:
- attended: bfloat16 [2048, 8, 8, 128], P('ctx', 'tp', 'section')
- query_grad: float32 [2048, 8, 8, 128], P('ctx', 'tp', 'section')
- key_grad: float32 [2048, 8, 128], P('ctx', 'tp')
- value_grad: float32 [2048, 8, 128], P('ctx', 'tp')
Inputs may be any that keep to these rules, and one draw needn't show every extreme that they name: `band_offsets`: in every row r the first offset is 0, the second lies in 1 to 2 and the third in 3 to 4; an offset larger than r is replaced by -1. `global_blocks`: entry n of row r is either -1 or n * 4, and it is n * 4 only when n * 4 < r - 4.
All inputs are finite; a program needn't handle non-finite values.
Results may differ from a plain program's by a relative error of at most 0.017.
Values may be sent and summed in bfloat16 or wider, within the bound.
A program may use at most 128 MiB of HBM per device.

v0:
```python
import jax
import jax.numpy as jnp
from jax import lax
from jax.sharding import PartitionSpec as P

BLK = 128
NBAND = 3
NGLOB = 4


def passed_along(shard, axis, by):
    count = lax.axis_size(axis)
    pairs = [(i, i + by) for i in range(count) if 0 <= i + by < count]
    return lax.ppermute(shard, axis, pairs)


def shards(queries, key_states, value_states, out_grad, band_offsets, global_blocks):
    tok_rows, kv_local, group_local, head_dim = queries.shape
    own_blocks = tok_rows // BLK
    ctx_count = lax.axis_size("ctx")
    all_blocks = own_blocks * ctx_count
    stride_blocks = all_blocks // NGLOB
    stride_devices = stride_blocks // own_blocks
    position = lax.axis_index("ctx")
    scale_factor = head_dim ** (-0.5)
    paired = jnp.stack([key_states, value_states])
    earlier = passed_along(paired, "ctx", 1)
    leading = paired[:, :BLK]
    every_first = lax.all_gather(leading, "ctx", axis=1, tiled=True)
    grouped = every_first.reshape(2, ctx_count, BLK, kv_local, head_dim)[:, ::stride_devices]
    global_rows = grouped.reshape(2, NGLOB * BLK, kv_local, head_dim)
    buffer_blocks = 2 * own_blocks + NGLOB
    stacked = jnp.concatenate([earlier, paired, global_rows], axis=1).reshape(
        2, buffer_blocks, BLK, kv_local, head_dim
    )
    offsets = lax.dynamic_slice_in_dim(band_offsets, position * own_blocks, own_blocks, 0)
    chosen_globals = lax.dynamic_slice_in_dim(global_blocks, position * own_blocks, own_blocks, 0)
    local_rows = jnp.arange(own_blocks, dtype=jnp.int32)[:, None]
    band_ids = own_blocks + local_rows - offsets
    glob_ids = 2 * own_blocks + chosen_globals // stride_blocks
    usable = jnp.concatenate([offsets >= 0, chosen_globals >= 0], axis=1)
    block_ids = jnp.where(usable, jnp.concatenate([band_ids, glob_ids], axis=1), 0)
    key_sel = stacked[0][block_ids]
    value_sel = stacked[1][block_ids]
    query_rows = queries.reshape(own_blocks, BLK, kv_local, group_local, head_dim)
    grad_rows = out_grad.reshape(own_blocks, BLK, kv_local, group_local, head_dim)
    scores = (
        jnp.einsum("rihgd,rnjhd->rhginj", query_rows, key_sel, preferred_element_type=jnp.float32)
        * scale_factor
    )
    lower_half = jnp.arange(BLK)[:, None] >= jnp.arange(BLK)[None, :]
    first_slot = jnp.arange(NBAND + NGLOB) == 0
    reach = jnp.logical_not(first_slot)[None, :, None] | lower_half[:, None, :]
    allowed = usable[:, None, None, None, :, None] & reach[None, None, None]
    scores = jnp.where(allowed, scores, -jnp.inf)
    row_top = jnp.max(scores, axis=(4, 5), keepdims=True)
    probs = jnp.exp(scores - row_top)
    row_total = jnp.sum(probs, axis=(4, 5), keepdims=True)
    weights = probs / row_total
    weights_low = weights.astype(jnp.bfloat16)
    attended = jnp.einsum(
        "rhginj,rnjhd->rihgd", weights_low, value_sel, preferred_element_type=jnp.float32
    ).astype(jnp.bfloat16)
    row_dots = jnp.sum(grad_rows.astype(jnp.float32) * attended.astype(jnp.float32), axis=-1)
    row_dots = jnp.transpose(row_dots, (0, 2, 3, 1))
    dweights = jnp.einsum(
        "rihgd,rnjhd->rhginj", grad_rows, value_sel, preferred_element_type=jnp.float32
    )
    dscores = (weights * (dweights - row_dots[..., None, None])).astype(jnp.bfloat16)
    query_grad = scale_factor * jnp.einsum(
        "rhginj,rnjhd->rihgd", dscores, key_sel, preferred_element_type=jnp.float32
    )
    key_part = scale_factor * jnp.einsum(
        "rhginj,rihgd->rnjhd", dscores, query_rows, preferred_element_type=jnp.float32
    )
    value_part = jnp.einsum(
        "rhginj,rihgd->rnjhd", weights_low, grad_rows, preferred_element_type=jnp.float32
    )
    slot_count = own_blocks * (NBAND + NGLOB)
    target_ids = jnp.where(usable, block_ids, buffer_blocks).reshape(slot_count)

    def place_blocks(part_grad):
        flat_grad = part_grad.reshape(slot_count, BLK, kv_local, head_dim)
        placed = jax.ops.segment_sum(flat_grad, target_ids, num_segments=buffer_blocks + 1)
        return placed[:buffer_blocks]

    block_grads = jnp.stack([place_blocks(key_part), place_blocks(value_part)])
    earlier_grads = block_grads[:, :own_blocks].reshape(2, tok_rows, kv_local, head_dim)
    own_grads = block_grads[:, own_blocks : 2 * own_blocks].reshape(2, tok_rows, kv_local, head_dim)
    global_grads = block_grads[:, 2 * own_blocks :]
    returned = passed_along(earlier_grads.astype(jnp.bfloat16), "ctx", -1).astype(
        earlier_grads.dtype
    )
    own_grads = own_grads + returned
    owner_mask = (jnp.arange(NGLOB) * stride_devices == position).astype(jnp.float32)
    summed = lax.psum(global_grads.astype(jnp.bfloat16), "ctx").astype(jnp.float32)
    owner_rows = jnp.einsum("g,cgjhd->cjhd", owner_mask, summed, precision=lax.Precision.HIGHEST)
    totals = lax.psum(
        jnp.concatenate([own_grads[:, :BLK] + owner_rows, own_grads[:, BLK:]], axis=1), "section"
    )
    return (
        attended.reshape(tok_rows, kv_local, group_local, head_dim),
        query_grad.reshape(tok_rows, kv_local, group_local, head_dim),
        totals[0],
        totals[1],
    )


def solution(mesh):
    placed = (
        P("ctx", "tp", "section", None),
        P("ctx", "tp", None),
        P("ctx", "tp", None),
        P("ctx", "tp", "section", None),
        P(),
        P(),
    )
    return jax.shard_map(
        shards,
        mesh=mesh,
        in_specs=placed,
        out_specs=(
            P("ctx", "tp", "section", None),
            P("ctx", "tp", "section", None),
            P("ctx", "tp", None),
            P("ctx", "tp", None),
        ),
        check_vma=False,
    )
```

profile of v0, /device:TPU:0, one launch (start us, length us, event | category | flops | bytes accessed | tf_op | source)
XLA Modules:
  0.0 332.9 jit_solution(10869660269288517391)
XLA Ops:
  7.3 1.5 copy_bitcast_fusion
  8.7 0.7 fusion.38
  9.5 1.1 pad_maximum_fusion.3
  10.6 6.0 %collective-permute-start = (bf16[2,512,4,128]{3,1,2,0:T(8,128)(2,1)}, bf16[2,512,4,128]{3,1,2,0:T(8,128)(2,1)}, u32[]{:S(2)}, u32[]{:S(2)}) collective-permute-start(bf16[2,512,4,128]{3,1,2,0:T(8,128)(2,1)} %pad_maximum_fusion.3), channel_id=1, source_target_pairs={{0,2},{2,4},{4,6},{1,3},{3,5},{5,7},{8,10},{10,12},{12,14},{9,11},... | collective-permute-start | bytes 3145736 | tf_op jit(solution)/shard_map/ppermute | solution.py:14
  17.4 1.1 copy.93
  19.2 0.3 broadcast_and_fusion
  19.4 35.7 %collective-permute-done = bf16[2,512,4,128]{3,1,2,0:T(8,128)(2,1)} collective-permute-done((bf16[2,512,4,128]{3,1,2,0:T(8,128)(2,1)}, bf16[2,512,4,128]{3,1,2,0:T(8,128)(2,1)}, u32[]{:S(2)}, u32[]{:S(2)}) %collective-permute-start) | collective-permute-done | bytes 1048608 | tf_op jit(solution)/shard_map/ppermute | solution.py:14
  55.1 1.6 pad_maximum_fusion.1
  56.8 1.3 fusion.46
  58.2 2.9 gather_fusion.1
  61.1 8.5 %fusion.4 = (f32[4,4,2,128]{3,2,1,0:T(2,128)S(1)}, f32[4,4,7,128,128,2]{4,3,5,2,1,0:T(8,128)}) fusion(pred[4,128,7,128]{1,3,2,0:T(8,128)(4,1)S(1)} %broadcast_and_fusion, bf16[4,128,4,2,128,1]{4,3,2,1,0,5:T(2,128)(2,1)S(1)} %bitcast.99, bf16[4,7,128,4,128,1]{4,2,3,1,0,5:T(8,128)(2,1)} %bitcast.110), kind=kOutput, calls=%fused_computation.11 | convolution fusion | flops 950530048 | bytes 19873792 | tf_op jit(solution)/shard_map/rihgd,rnjhd->rhginj/dot_general | solution.py:48
  69.5 8.2 %fusion.3 = f32[4,4,2,128]{3,2,1,0:T(2,128)S(1)} fusion(f32[4,4,7,128,128,2]{4,3,5,2,1,0:T(8,128)} %get-tuple-element.23, f32[4,4,2,128]{3,2,1,0:T(2,128)S(1)} %get-tuple-element.22, pred[4,128,7,128]{1,3,2,0:T(8,128)(4,1)S(1)} %broadcast_and_fusion), kind=kLoop, calls=%fused_computation.10 | loop fusion | flops 14675968 | bytes 15171584 | tf_op jit(solution)/shard_map/reduce_sum | solution.py:58
  77.8 9.6 %fusion.16 = bf16[4,4,2,128,7,128]{3,5,2,4,1,0:T(8,128)(2,1)} fusion(f32[4,4,2,128]{3,2,1,0:T(2,128)S(1)} %fusion.3, f32[4,4,2,128]{3,2,1,0:T(2,128)S(1)} %get-tuple-element.22, f32[4,4,7,128,128,2]{4,3,5,2,1,0:T(8,128)} %get-tuple-element.23, pred[4,128,7,128]{1,3,2,0:T(8,128)(4,1)S(1)} %broadcast_and_fusion), kind=kLoop, calls=%fused_computation.31 | loop fusion | flops 18350080 | bytes 22511616 | tf_op jit(solution)/shard_map/convert_element_type | solution.py:60
  87.5 2.9 gather_fusion
  90.4 8.5 %convolution_bitcast_fusion = f32[4,7,128,4,128]{4,2,1,3,0:T(8,128)} fusion(bf16[4,4,2,128,7,128]{3,5,2,4,1,0:T(8,128)(2,1)} %fusion.16, bf16[4,128,4,2,128,1]{4,1,0,3,2,5:T(8,128)(2,1)} %bitcast.107), kind=kOutput, calls=%fused_computation.30 | convolution fusion | flops 939524096 | bytes 15728640 | tf_op jit(solution)/shard_map/rhginj,rihgd->rnjhd/dot_general | solution.py:76
  98.8 6.6 %multiply_reduce_fusion = (f32[4,128,4,2]{1,3,2,0:T(2,128)S(1)}, bf16[4,128,4,2,128]{4,1,3,2,0:T(8,128)(2,1)}) fusion(bf16[4,128,4,2,128]{4,1,0,3,2:T(8,128)(2,1)S(1)} %bitcast.108, bf16[4,4,2,128,7,128]{3,5,2,4,1,0:T(8,128)(2,1)} %fusion.16, bf16[4,7,128,4,128,1]{4,2,3,1,0,5:T(8,128)(2,1)S(1)} %bitcast.112), kind=kOutput, calls=%fused_computation.38 | convolution fusion | flops 942141440 | bytes 13123584 | tf_op jit(solution)/shard_map/rhginj,rnjhd->rihgd/dot_general | solution.py:61
  105.5 8.0 %fusion.1 = bf16[4,4,2,128,7,128]{3,5,2,4,1,0:T(8,128)(2,1)S(1)} fusion(f32[4,4,2,128]{3,2,1,0:T(2,128)S(1)} %bitcast.119, bf16[4,7,128,4,128,1]{4,2,3,1,0,5:T(8,128)(2,1)S(1)} %bitcast.113, f32[4,4,2,128]{3,2,1,0:T(2,128)S(1)} %fusion.3, f32[4,4,2,128]{3,2,1,0:T(2,128)S(1)} %get-tuple-element.22, f32[4,4,7,128,128,2]{4,3,5,2,1,0:T(8,128)} %get-tuple-element.23, ...), kind=kOutput, calls=%fused_computation.6 | convolution fusion | flops 965214208 | bytes 27246592 | tf_op jit(solution)/shard_map/rihgd,rnjhd->rhginj/dot_general | solution.py:66
  113.5 2.1 fusion.5
  115.6 0.8 copy-done.4
  116.4 4.0 %copy.103 = f32[4,7,128,4,128]{4,2,3,1,0:T(8,128)} copy(f32[4,7,128,4,128]{4,2,1,3,0:T(8,128)S(1)} %fusion.5) | data formatting | bytes 14680064 | tf_op jit(solution)/shard_map/mul | solution.py:73
  120.4 2.2 broadcast.117.clone
  122.6 17.9 %scatter_fusion = f32[13,128,4,128]{3,1,2,0:T(8,128)} fusion(f32[13,128,4,128]{3,1,2,0:T(8,128)} %broadcast.117.clone, s32[28]{0:T(128)S(1)} %fusion.42, f32[28,128,4,128]{3,1,2,0:T(8,128)} %bitcast.102), kind=kCustom, calls=%fused_computation.2 | custom fusion | flops 1835008 | bytes 22020208 | tf_op jit(solution)/shard_map/scatter-add | solution.py:84
  140.5 3.9 %slice_bitcast_fusion.1 = f32[1,12,128,4,128]{4,2,3,1,0:T(8,128)} fusion(f32[13,128,4,128]{3,1,2,0:T(8,128)} %scatter_fusion), kind=kLoop, calls=%fused_computation.28 | loop fusion | bytes 6291456 | tf_op jit(solution)/shard_map/stack | solution.py:87
  144.4 7.0 %copy.105 = f32[4,7,128,4,128]{4,2,3,1,0:T(8,128)} copy(f32[4,7,128,4,128]{4,2,1,3,0:T(8,128)} %convolution_bitcast_fusion) | data formatting | bytes 14680064 | tf_op jit(solution)/shard_map/rhginj,rihgd->rnjhd/transpose | solution.py:76
  151.5 2.1 broadcast.117.clone.1
  153.6 17.2 %scatter_fusion.1 = f32[13,128,4,128]{3,1,2,0:T(8,128)} fusion(f32[13,128,4,128]{3,1,2,0:T(8,128)} %broadcast.117.clone.1, s32[28]{0:T(128)S(1)} %fusion.42, f32[28,128,4,128]{3,1,2,0:T(8,128)} %bitcast.101), kind=kCustom, calls=%fused_computation.3 | custom fusion | flops 1835008 | bytes 22020208 | tf_op jit(solution)/shard_map/scatter-add | solution.py:84
  170.8 2.2 slice_bitcast_fusion
  173.0 0.6 copy-done.2
  173.6 0.6 fusion.10
  174.2 1.1 copy-done.3
  175.3 1.1 fusion.45
  176.5 1.3 collective-permute-start.1
  177.8 0.3 all-reduce.5.cloned.1.call-start
  178.1 1.7 fusion.17
  179.8 0.2 copy.106
  180.0 40.9 %collective-permute-done.1 = bf16[2,512,4,128]{3,1,2,0:T(8,128)(2,1)S(1)} collective-permute-done((bf16[2,512,4,128]{3,1,2,0:T(8,128)(2,1)S(1)}, bf16[2,512,4,128]{3,1,2,0:T(8,128)(2,1)S(1)}, u32[]{:S(2)}, u32[]{:S(2)}) %collective-permute-start.1) | collective-permute-done | bytes 1048608 | tf_op jit(solution)/shard_map/ppermute | solution.py:14
  220.9 0.2 bitcast_add_fusion
  221.1 1.3 slice.67
  222.4 26.3 %all-reduce.3.cloned.1.call-done = bf16[2,4,128,4,128]{4,2,3,1,0:T(8,128)(2,1)} async-done(((bf16[2,4,128,4,128]{4,2,3,1,0:T(8,128)(2,1)}), bf16[2,4,128,4,128]{4,2,3,1,0:T(8,128)(2,1)}) %all-reduce.3.cloned.1.call-update) | async-done | bytes 1048592 | tf_op jit(solution)/shard_map/psum | solution.py:96
  248.7 2.2 fusion.32
  251.0 1.5 pad_maximum_fusion.2
  252.7 2.0 copy.108
  254.7 5.9 %fusion.18 = f32[4,128,4,2,128]{4,1,3,2,0:T(8,128)S(1)} fusion(bf16[4,4,2,128,7,128]{3,5,2,4,1,0:T(8,128)(2,1)} %copy-done.4, bf16[4,7,128,4,128,1]{4,2,3,1,0,5:T(8,128)(2,1)S(1)} %bitcast.111), kind=kOutput, calls=%fused_computation.36 | convolution fusion | flops 940048384 | bytes 13107200 | tf_op jit(solution)/shard_map/rhginj,rnjhd->rihgd/dot_general | solution.py:70
  260.9 2.9 copy.109
  263.8 57.6 %all-reduce.5.cloned.1.call-done = f32[2,512,4,128]{3,1,2,0:T(8,128)} async-done(((f32[2,512,4,128]{3,1,2,0:T(8,128)}), f32[2,512,4,128]{3,1,2,0:T(8,128)}) %all-reduce.5.cloned.1.call-update) | async-done | bytes 2097168 | tf_op jit(solution)/shard_map/psum | solution.py:98
  321.4 1.7 slice_bitcast_fusion.2
  323.1 1.6 copy.110
  324.8 1.6 copy.111
  (59 shorter events, 2.3 us)
Async XLA Ops:
  7.2 53.9 %copy-start = (bf16[512,4,2,128]{3,2,1,0:T(2,128)(2,1)S(1)}, bf16[512,4,2,128]{3,2,1,0:T(2,128)(2,1)}, u32[]{:S(2)}) copy-start(bf16[512,4,2,128]{3,2,1,0:T(2,128)(2,1)} %param.6) | copy-start | bytes 3145732
  7.2 9.4 %copy-start.12 = (s32[16,4]{0,1:T(4,128)S(1)}, s32[16,4]{0,1:T(4,128)}, u32[]{:S(2)}) copy-start(s32[16,4]{0,1:T(4,128)} %param.11) | copy-start | bytes 772
  7.2 9.6 %copy-start.13 = (s32[16,3]{0,1:T(4,128)S(1)}, s32[16,3]{0,1:T(4,128)}, u32[]{:S(2)}) copy-start(s32[16,3]{0,1:T(4,128)} %param.10) | copy-start | bytes 580
  7.2 10.2 %copy-start.10 = (bf16[512,4,2,128]{3,2,1,0:T(2,128)(2,1)S(1)}, bf16[512,4,2,128]{3,2,1,0:T(2,128)(2,1)}, u32[]{:S(2)}) copy-start(bf16[512,4,2,128]{3,2,1,0:T(2,128)(2,1)} %param.9) | copy-start | bytes 3145732
  7.2 47.9 %all-gather.2.cloned.1.call-start = ((), (), s32[]{:S(2)}) async-start(), calls=%async_computation | async-start | bytes 1310720 | tf_op jit(solution)/shard_map/all_gather | solution.py:29
  9.5 239.2 %all-reduce.3.cloned.1.call-start = ((), (), s32[]{:S(2)}) async-start(), calls=%async_computation.1 | async-start | bytes 2097152 | tf_op jit(solution)/shard_map/psum | solution.py:96
  10.6 44.5 %collective-permute-start = (bf16[2,512,4,128]{3,1,2,0:T(8,128)(2,1)}, bf16[2,512,4,128]{3,1,2,0:T(8,128)(2,1)}, u32[]{:S(2)}, u32[]{:S(2)}) collective-permute-start(bf16[2,512,4,128]{3,1,2,0:T(8,128)(2,1)} %pad_maximum_fusion.3), channel_id=1, source_target_pairs={{0,2},{2,4},{4,6},{1,3},{3,5},{5,7},{8,10},{10,12},{12,14},{9,11},... | collective-permute-start | bytes 3145736 | tf_op jit(solution)/shard_map/ppermute | solution.py:14
  77.8 9.6 %copy-start.5 = (bf16[1,1536,4,128]{3,1,2,0:T(8,128)(2,1)S(1)}, bf16[1,1536,4,128]{3,1,2,0:T(8,128)(2,1)}, u32[]{:S(2)}) copy-start(bf16[1,1536,4,128]{3,1,2,0:T(8,128)(2,1)} %get-tuple-element.18) | copy-start | bytes 4718596
  90.4 8.5 %copy-start.7 = (bf16[512,4,2,128]{3,0,2,1:T(8,128)(2,1)S(1)}, bf16[512,4,2,128]{3,0,2,1:T(8,128)(2,1)}, u32[]{:S(2)}) copy-start(bf16[512,4,2,128]{3,0,2,1:T(8,128)(2,1)} %copy.93) | copy-start | bytes 3145732
  90.4 8.5 %copy-start.9 = (bf16[28,128,4,128]{3,1,2,0:T(8,128)(2,1)S(1)}, bf16[28,128,4,128]{3,1,2,0:T(8,128)(2,1)}, u32[]{:S(2)}) copy-start(bf16[28,128,4,128]{3,1,2,0:T(8,128)(2,1)} %gather_fusion) | copy-start | bytes 11010052
  113.5 2.9 copy-start.4
  170.8 2.8 copy-start.2
  173.6 1.7 copy-start.3
  176.5 44.4 %collective-permute-start.1 = (bf16[2,512,4,128]{3,1,2,0:T(8,128)(2,1)S(1)}, bf16[2,512,4,128]{3,1,2,0:T(8,128)(2,1)S(1)}, u32[]{:S(2)}, u32[]{:S(2)}) collective-permute-start(bf16[2,512,4,128]{3,1,2,0:T(8,128)(2,1)S(1)} %bitcast.114), channel_id=1, source_target_pairs={{2,0},{4,2},{6,4},{3,1},{5,3},{7,5},{10,8},{12,10},{14,12},{11,9},... | collective-permute-start | bytes 3145736 | tf_op jit(solution)/shard_map/ppermute | solution.py:14
  177.8 143.6 %all-reduce.5.cloned.1.call-start = ((), (), s32[]{:S(2)}) async-start(), calls=%async_computation.2 | async-start | bytes 4194304 | tf_op jit(solution)/shard_map/psum | solution.py:98
  248.7 2.3 copy-start.6
  251.0 1.6 copy-start.11
  252.5 2.2 copy-start.8
  260.8 65.6 %copy-start.1 = (bf16[512,4,2,128]{3,2,1,0:T(2,128)(2,1)S(1)}, bf16[512,4,2,128]{3,2,1,0:T(2,128)(2,1)}, u32[]{:S(2)}) copy-start(bf16[512,4,2,128]{3,2,1,0:T(2,128)(2,1)} %param.6) | copy-start | bytes 3145732
Sparse Core Ops, SparseCore 0:
  10.2 44.1 all-gather.1
  177.9 70.7 all-reduce.2
  252.6 68.7 all-reduce.4
where the time goes:
time: 334 us; the launch traced here: 333 us
  waiting for transfers between devices  161 us (48%)
  other arithmetic  61.2 us (18%)
  local copies, waits for them, and re-layouts  47.8 us (14%)
  matrix products  41.8 us (13%)
  between operations  14 us (4%)
  starting transfers between devices  7.61 us (2%)
    ppermute x2, waiting for transfers between devices, passed_along(): return lax.ppermute(shard, axis, pairs)  76.6 us
    psum x1, waiting for transfers between devices, shards(): lax.psum(jnp.concatenate([own_grads[:, :BLK] + owner_rows, own_grads[:, B...  57.6 us
    scatter-add x2, other arithmetic, place_blocks(): jax.ops.segment_sum(flat_grad, target_ids, num_segments=buffer_blocks + 1)  35 us
    psum x1, waiting for transfers between devices, shards(): lax.psum(global_grads.astype(jnp.bfloat16), 'ctx').astype(jnp.float32)  26.3 us
    unnamed x33, local copies, waits for them, and re-layouts  12 us
    convert_element_type x1, other arithmetic, shards(): weights_low = weights.astype(jnp.bfloat16)  9.61 us
    dot_general x1, matrix products, shards(): jnp.einsum('rihgd,rnjhd->rhginj', query_rows, key_sel, preferred_element_...  8.46 us
    dot_general x1, matrix products, shards(): jnp.einsum('rhginj,rihgd->rnjhd', weights_low, grad_rows, preferred_eleme...  8.45 us
  transfers between devices with their start and end apart: 5, of which 4 were waited for; matrix products, arithmetic and copies ran while one was open for 6% of the time, Pallas kernels for 0%

commit v1 on v0

--- a/solution.py
+++ b/solution.py
@@ -1,3 +1,4 @@
+import functools
 import jax
 import jax.numpy as jnp
 from jax import lax
@@ -6,6 +7,14 @@
 BLK = 128
 NBAND = 3
 NGLOB = 4
+
+
+def move_the_lanes(target, axis_key):
+    outer = jax.lax.all_gather(target, axis_key)
+    return jnp.sum(outer, 0)
+
+
+prepare_figure = functools.partial(move_the_lanes, axis_key="section")
 
 
 def passed_along(shard, axis, by):
@@ -95,8 +104,8 @@
     owner_mask = (jnp.arange(NGLOB) * stride_devices == position).astype(jnp.float32)
     summed = lax.psum(global_grads.astype(jnp.bfloat16), "ctx").astype(jnp.float32)
     owner_rows = jnp.einsum("g,cgjhd->cjhd", owner_mask, summed, precision=lax.Precision.HIGHEST)
-    totals = lax.psum(
-        jnp.concatenate([own_grads[:, :BLK] + owner_rows, own_grads[:, BLK:]], axis=1), "section"
+    totals = prepare_figure(
+        jnp.concatenate([own_grads[:, :BLK] + owner_rows, own_grads[:, BLK:]], axis=1)
     )
     return (
         attended.reshape(tok_rows, kv_local, group_local, head_dim),

time: 334 us -> 354 us (1.060)
  waiting for transfers between devices: 161 us -> 179 us
  other arithmetic: 61.2 us -> 65.2 us
    all_gather x0 -> x1, waiting for transfers between devices: none -> 76.1 us  [move_the_lanes(): outer = jax.lax.all_gather(target, axis_key)]
    psum x1 -> x0, waiting for transfers between devices: 57.6 us -> none  [shards(): lax.psum(jnp.concatenate([own_grads[:, :BLK] + owner_rows, own_grads[:, B...]
    reduce_sum x0 -> x1, other arithmetic: none -> 4.16 us  [move_the_lanes(): return jnp.sum(outer, 0)]
  transfers between devices with their start and end apart: 5 -> 5, of which waited for: 4 -> 4; matrix products, arithmetic and copies ran while one was open for 6% -> 5% of each run, Pallas kernels for 0% -> 0%
where the time goes in v1:
time: 354 us
  waiting for transfers between devices  179 us (51%)
  other arithmetic  65.2 us (18%)
  local copies, waits for them, and re-layouts  46.2 us (13%)
  matrix products  41.4 us (12%)
  between operations  14 us (4%)
  starting transfers between devices  7.61 us (2%)
    ppermute x2, waiting for transfers between devices, passed_along(): return lax.ppermute(shard, axis, pairs)  77 us
    all_gather x1, waiting for transfers between devices, move_the_lanes(): outer = jax.lax.all_gather(target, axis_key)  76.1 us
    scatter-add x2, other arithmetic, place_blocks(): jax.ops.segment_sum(flat_grad, target_ids, num_segments=buffer_blocks + 1)  34.8 us
    psum x1, waiting for transfers between devices, shards(): lax.psum(global_grads.astype(jnp.bfloat16), 'ctx').astype(jnp.float32)  26.3 us
    unnamed x33, local copies, waits for them, and re-layouts  12.1 us
    convert_element_type x1, other arithmetic, shards(): weights_low = weights.astype(jnp.bfloat16)  9.59 us
    dot_general x1, matrix products, shards(): jnp.einsum('rhginj,rihgd->rnjhd', weights_low, grad_rows, preferred_eleme...  8.53 us
    dot_general x1, matrix products, shards(): jnp.einsum('rihgd,rnjhd->rhginj', query_rows, key_sel, preferred_element_...  8.51 us
  transfers between devices with their start and end apart: 5, of which 4 were waited for; matrix products, arithmetic and copies ran while one was open for 5% of the time, Pallas kernels for 0%

profile of v1, /device:TPU:0, one launch (start us, length us, event | category | flops | bytes accessed | tf_op | source)
XLA Modules:
  0.0 353.9 jit_solution(17239822524331131653)
XLA Ops:
  7.3 1.5 copy_bitcast_fusion
  8.7 0.7 fusion.38
  9.5 1.1 pad_maximum_fusion.3
  10.6 6.0 %collective-permute-start = (bf16[2,512,4,128]{3,1,2,0:T(8,128)(2,1)}, bf16[2,512,4,128]{3,1,2,0:T(8,128)(2,1)}, u32[]{:S(2)}, u32[]{:S(2)}) collective-permute-start(bf16[2,512,4,128]{3,1,2,0:T(8,128)(2,1)} %pad_maximum_fusion.3), channel_id=1, source_target_pairs={{0,2},{2,4},{4,6},{1,3},{3,5},{5,7},{8,10},{10,12},{12,14},{9,11},... | collective-permute-start | bytes 3145736 | tf_op jit(solution)/shard_map/ppermute | solution.py:23
  17.4 1.1 copy.120
  19.2 0.3 broadcast_and_fusion
  19.4 35.7 %collective-permute-done = bf16[2,512,4,128]{3,1,2,0:T(8,128)(2,1)} collective-permute-done((bf16[2,512,4,128]{3,1,2,0:T(8,128)(2,1)}, bf16[2,512,4,128]{3,1,2,0:T(8,128)(2,1)}, u32[]{:S(2)}, u32[]{:S(2)}) %collective-permute-start) | collective-permute-done | bytes 1048608 | tf_op jit(solution)/shard_map/ppermute | solution.py:23
  55.1 1.6 pad_maximum_fusion.1
  56.8 1.3 fusion.46
  58.2 2.9 gather_fusion.1
  61.1 8.5 %fusion.4 = (f32[4,4,2,128]{3,2,1,0:T(2,128)S(1)}, f32[4,4,7,128,128,2]{4,3,5,2,1,0:T(8,128)}) fusion(pred[4,128,7,128]{1,3,2,0:T(8,128)(4,1)S(1)} %broadcast_and_fusion, bf16[4,128,4,2,128,1]{4,3,2,1,0,5:T(2,128)(2,1)S(1)} %bitcast.100, bf16[4,7,128,4,128,1]{4,2,3,1,0,5:T(8,128)(2,1)} %bitcast.112), kind=kOutput, calls=%fused_computation.11 | convolution fusion | flops 950530048 | bytes 19873792 | tf_op jit(solution)/shard_map/rihgd,rnjhd->rhginj/dot_general | solution.py:57
  69.6 8.2 %fusion.3 = f32[4,4,2,128]{3,2,1,0:T(2,128)S(1)} fusion(f32[4,4,7,128,128,2]{4,3,5,2,1,0:T(8,128)} %get-tuple-element.27, f32[4,4,2,128]{3,2,1,0:T(2,128)S(1)} %get-tuple-element.26, pred[4,128,7,128]{1,3,2,0:T(8,128)(4,1)S(1)} %broadcast_and_fusion), kind=kLoop, calls=%fused_computation.10 | loop fusion | flops 14675968 | bytes 15171584 | tf_op jit(solution)/shard_map/reduce_sum | solution.py:67
  77.9 9.6 %fusion.16 = bf16[4,4,2,128,7,128]{3,5,2,4,1,0:T(8,128)(2,1)} fusion(f32[4,4,2,128]{3,2,1,0:T(2,128)S(1)} %fusion.3, f32[4,4,2,128]{3,2,1,0:T(2,128)S(1)} %get-tuple-element.26, f32[4,4,7,128,128,2]{4,3,5,2,1,0:T(8,128)} %get-tuple-element.27, pred[4,128,7,128]{1,3,2,0:T(8,128)(4,1)S(1)} %broadcast_and_fusion), kind=kLoop, calls=%fused_computation.31 | loop fusion | flops 18350080 | bytes 22511616 | tf_op jit(solution)/shard_map/convert_element_type | solution.py:69
  87.6 2.9 gather_fusion
  90.4 8.5 %convolution_bitcast_fusion = f32[4,7,128,4,128]{4,2,1,3,0:T(8,128)} fusion(bf16[4,4,2,128,7,128]{3,5,2,4,1,0:T(8,128)(2,1)} %fusion.16, bf16[4,128,4,2,128,1]{4,1,0,3,2,5:T(8,128)(2,1)} %bitcast.109), kind=kOutput, calls=%fused_computation.30 | convolution fusion | flops 939524096 | bytes 15728640 | tf_op jit(solution)/shard_map/rhginj,rihgd->rnjhd/dot_general | solution.py:85
  99.0 6.6 %multiply_reduce_fusion = (f32[4,128,4,2]{1,3,2,0:T(2,128)S(1)}, bf16[4,128,4,2,128]{4,1,3,2,0:T(8,128)(2,1)}) fusion(bf16[4,128,4,2,128]{4,1,0,3,2:T(8,128)(2,1)S(1)} %bitcast.110, bf16[4,4,2,128,7,128]{3,5,2,4,1,0:T(8,128)(2,1)} %fusion.16, bf16[4,7,128,4,128,1]{4,2,3,1,0,5:T(8,128)(2,1)S(1)} %bitcast.114), kind=kOutput, calls=%fused_computation.38 | convolution fusion | flops 942141440 | bytes 13123584 | tf_op jit(solution)/shard_map/rhginj,rnjhd->rihgd/dot_general | solution.py:70
  105.6 8.0 %fusion.1 = bf16[4,4,2,128,7,128]{3,5,2,4,1,0:T(8,128)(2,1)S(1)} fusion(f32[4,4,2,128]{3,2,1,0:T(2,128)S(1)} %bitcast.121, bf16[4,7,128,4,128,1]{4,2,3,1,0,5:T(8,128)(2,1)S(1)} %bitcast.115, f32[4,4,2,128]{3,2,1,0:T(2,128)S(1)} %fusion.3, f32[4,4,2,128]{3,2,1,0:T(2,128)S(1)} %get-tuple-element.26, f32[4,4,7,128,128,2]{4,3,5,2,1,0:T(8,128)} %get-tuple-element.27, ...), kind=kOutput, calls=%fused_computation.6 | convolution fusion | flops 965214208 | bytes 27246592 | tf_op jit(solution)/shard_map/rihgd,rnjhd->rhginj/dot_general | solution.py:75
  113.6 2.1 fusion.5
  115.7 0.9 copy-done.4
  116.7 4.0 %copy.130 = f32[4,7,128,4,128]{4,2,3,1,0:T(8,128)} copy(f32[4,7,128,4,128]{4,2,1,3,0:T(8,128)S(1)} %fusion.5) | data formatting | bytes 14680064 | tf_op jit(solution)/shard_map/mul | solution.py:82
  120.6 2.1 broadcast.117.clone
  122.8 17.6 %scatter_fusion = f32[13,128,4,128]{3,1,2,0:T(8,128)} fusion(f32[13,128,4,128]{3,1,2,0:T(8,128)} %broadcast.117.clone, s32[28]{0:T(128)S(1)} %fusion.42, f32[28,128,4,128]{3,1,2,0:T(8,128)} %bitcast.103), kind=kCustom, calls=%fused_computation.2 | custom fusion | flops 1835008 | bytes 22020208 | tf_op jit(solution)/shard_map/scatter-add | solution.py:93
  140.4 3.9 %slice_bitcast_fusion.1 = f32[1,12,128,4,128]{4,2,3,1,0:T(8,128)} fusion(f32[13,128,4,128]{3,1,2,0:T(8,128)} %scatter_fusion), kind=kLoop, calls=%fused_computation.28 | loop fusion | bytes 6291456 | tf_op jit(solution)/shard_map/stack | solution.py:96
  144.3 7.0 %copy.132 = f32[4,7,128,4,128]{4,2,3,1,0:T(8,128)} copy(f32[4,7,128,4,128]{4,2,1,3,0:T(8,128)} %convolution_bitcast_fusion) | data formatting | bytes 14680064 | tf_op jit(solution)/shard_map/rhginj,rihgd->rnjhd/transpose | solution.py:85
  151.3 2.2 broadcast.117.clone.1
  153.5 17.2 %scatter_fusion.1 = f32[13,128,4,128]{3,1,2,0:T(8,128)} fusion(f32[13,128,4,128]{3,1,2,0:T(8,128)} %broadcast.117.clone.1, s32[28]{0:T(128)S(1)} %fusion.42, f32[28,128,4,128]{3,1,2,0:T(8,128)} %bitcast.102), kind=kCustom, calls=%fused_computation.3 | custom fusion | flops 1835008 | bytes 22020208 | tf_op jit(solution)/shard_map/scatter-add | solution.py:93
  170.7 2.2 slice_bitcast_fusion
  172.9 0.6 copy-done.2
  173.5 0.6 fusion.10
  174.1 1.1 copy-done.3
  175.3 1.1 fusion.45
  176.4 1.3 collective-permute-start.1
  177.8 0.3 all-gather.6.cloned.1.call-start
  178.0 1.7 fusion.17
  179.7 0.2 copy.133
  179.9 41.3 %collective-permute-done.1 = bf16[2,512,4,128]{3,1,2,0:T(8,128)(2,1)S(1)} collective-permute-done((bf16[2,512,4,128]{3,1,2,0:T(8,128)(2,1)S(1)}, bf16[2,512,4,128]{3,1,2,0:T(8,128)(2,1)S(1)}, u32[]{:S(2)}, u32[]{:S(2)}) %collective-permute-start.1) | collective-permute-done | bytes 1048608 | tf_op jit(solution)/shard_map/ppermute | solution.py:23
  221.2 0.2 bitcast_add_fusion
  221.5 1.3 slice.67
  222.7 26.3 %all-reduce.2.cloned.1.call-done = bf16[2,4,128,4,128]{4,2,3,1,0:T(8,128)(2,1)} async-done(((bf16[2,4,128,4,128]{4,2,3,1,0:T(8,128)(2,1)}), bf16[2,4,128,4,128]{4,2,3,1,0:T(8,128)(2,1)}) %all-reduce.2.cloned.1.call-update) | async-done | bytes 1048592 | tf_op jit(solution)/shard_map/psum | solution.py:105
  249.0 2.2 fusion.32
  251.4 1.5 pad_maximum_fusion.2
  253.0 2.0 copy.135
  255.1 5.4 %fusion.18 = f32[4,128,4,2,128]{4,1,3,2,0:T(8,128)S(1)} fusion(bf16[4,4,2,128,7,128]{3,5,2,4,1,0:T(8,128)(2,1)} %copy-done.4, bf16[4,7,128,4,128,1]{4,2,3,1,0,5:T(8,128)(2,1)S(1)} %bitcast.113), kind=kOutput, calls=%fused_computation.36 | convolution fusion | flops 940048384 | bytes 13107200 | tf_op jit(solution)/shard_map/rhginj,rnjhd->rihgd/dot_general | solution.py:79
  260.7 2.9 copy.136
  263.6 76.1 %all-gather.6.cloned.1.call-done = f32[8,512,4,128]{3,1,2,0:T(8,128)} async-done(((f32[2,512,4,128]{3,1,2,0:T(8,128)}), f32[8,512,4,128]{3,1,2,0:T(8,128)}) %all-gather.6.cloned.1.call-update) | async-done | bytes 8388624 | tf_op jit(solution)/shard_map/all_gather | solution.py:13
  339.8 4.2 %reduce_sum.29 = f32[2,512,4,128]{3,1,2,0:T(8,128)S(1)} reduce(f32[4,2,512,4,128]{4,2,3,1,0:T(8,128)} %bitcast.104, f32[]{:T(128)} %constant.44.clone.1), dimensions={0}, to_apply=%region_6.7 | reduce | flops 1572864 | bytes 10485764 | tf_op jit(solution)/shard_map/reduce_sum | solution.py:14
  344.1 1.6 copy.137
  345.7 1.6 copy.138
  (60 shorter events, 2.4 us)
Async XLA Ops:
  7.2 53.9 %copy-start = (bf16[512,4,2,128]{3,2,1,0:T(2,128)(2,1)S(1)}, bf16[512,4,2,128]{3,2,1,0:T(2,128)(2,1)}, u32[]{:S(2)}) copy-start(bf16[512,4,2,128]{3,2,1,0:T(2,128)(2,1)} %param.6) | copy-start | bytes 3145732
  7.2 9.4 %copy-start.12 = (s32[16,4]{0,1:T(4,128)S(1)}, s32[16,4]{0,1:T(4,128)}, u32[]{:S(2)}) copy-start(s32[16,4]{0,1:T(4,128)} %param.11) | copy-start | bytes 772
  7.2 9.6 %copy-start.13 = (s32[16,3]{0,1:T(4,128)S(1)}, s32[16,3]{0,1:T(4,128)}, u32[]{:S(2)}) copy-start(s32[16,3]{0,1:T(4,128)} %param.10) | copy-start | bytes 580
  7.2 10.2 %copy-start.10 = (bf16[512,4,2,128]{3,2,1,0:T(2,128)(2,1)S(1)}, bf16[512,4,2,128]{3,2,1,0:T(2,128)(2,1)}, u32[]{:S(2)}) copy-start(bf16[512,4,2,128]{3,2,1,0:T(2,128)(2,1)} %param.9) | copy-start | bytes 3145732
  7.2 47.9 %all-gather.4.cloned.1.call-start = ((), (), s32[]{:S(2)}) async-start(), calls=%async_computation | async-start | bytes 1310720 | tf_op jit(solution)/shard_map/all_gather | solution.py:38
  9.5 239.5 %all-reduce.2.cloned.1.call-start = ((), (), s32[]{:S(2)}) async-start(), calls=%async_computation.1 | async-start | bytes 2097152 | tf_op jit(solution)/shard_map/psum | solution.py:105
  10.6 44.5 %collective-permute-start = (bf16[2,512,4,128]{3,1,2,0:T(8,128)(2,1)}, bf16[2,512,4,128]{3,1,2,0:T(8,128)(2,1)}, u32[]{:S(2)}, u32[]{:S(2)}) collective-permute-start(bf16[2,512,4,128]{3,1,2,0:T(8,128)(2,1)} %pad_maximum_fusion.3), channel_id=1, source_target_pairs={{0,2},{2,4},{4,6},{1,3},{3,5},{5,7},{8,10},{10,12},{12,14},{9,11},... | collective-permute-start | bytes 3145736 | tf_op jit(solution)/shard_map/ppermute | solution.py:23
  77.9 9.6 %copy-start.5 = (bf16[1,1536,4,128]{3,1,2,0:T(8,128)(2,1)S(1)}, bf16[1,1536,4,128]{3,1,2,0:T(8,128)(2,1)}, u32[]{:S(2)}) copy-start(bf16[1,1536,4,128]{3,1,2,0:T(8,128)(2,1)} %get-tuple-element.22) | copy-start | bytes 4718596
  90.4 8.5 %copy-start.7 = (bf16[512,4,2,128]{3,0,2,1:T(8,128)(2,1)S(1)}, bf16[512,4,2,128]{3,0,2,1:T(8,128)(2,1)}, u32[]{:S(2)}) copy-start(bf16[512,4,2,128]{3,0,2,1:T(8,128)(2,1)} %copy.120) | copy-start | bytes 3145732
  90.4 8.5 %copy-start.9 = (bf16[28,128,4,128]{3,1,2,0:T(8,128)(2,1)S(1)}, bf16[28,128,4,128]{3,1,2,0:T(8,128)(2,1)}, u32[]{:S(2)}) copy-start(bf16[28,128,4,128]{3,1,2,0:T(8,128)(2,1)} %gather_fusion) | copy-start | bytes 11010052
  113.6 3.0 copy-start.4
  170.7 2.8 copy-start.2
  173.5 1.7 copy-start.3
  176.4 44.8 %collective-permute-start.1 = (bf16[2,512,4,128]{3,1,2,0:T(8,128)(2,1)S(1)}, bf16[2,512,4,128]{3,1,2,0:T(8,128)(2,1)S(1)}, u32[]{:S(2)}, u32[]{:S(2)}) collective-permute-start(bf16[2,512,4,128]{3,1,2,0:T(8,128)(2,1)S(1)} %bitcast.116), channel_id=1, source_target_pairs={{2,0},{4,2},{6,4},{3,1},{5,3},{7,5},{10,8},{12,10},{14,12},{11,9},... | collective-permute-start | bytes 3145736 | tf_op jit(solution)/shard_map/ppermute | solution.py:23
  177.8 162.0 %all-gather.6.cloned.1.call-start = ((), (), s32[]{:S(2)}) async-start(), calls=%async_computation.2 | async-start | bytes 10485760 | tf_op jit(solution)/shard_map/all_gather | solution.py:13
  249.0 2.3 copy-start.6
  251.4 1.6 copy-start.11
  252.9 2.2 copy-start.8
  339.8 7.6 %copy-start.1 = (bf16[512,4,2,128]{3,2,1,0:T(2,128)(2,1)S(1)}, bf16[512,4,2,128]{3,2,1,0:T(2,128)(2,1)}, u32[]{:S(2)}) copy-start(bf16[512,4,2,128]{3,2,1,0:T(2,128)(2,1)} %param.6) | copy-start | bytes 3145732
Sparse Core Ops, SparseCore 0:
  10.2 44.1 all-gather.3
  177.9 71.0 all-reduce.1
  253.0 86.7 all-gather.5
